TPU v7x, 128 devices: a whole 4x4x4 slice. The times are simulated.
128 devices in a mesh: box: 16 (over x, y_lo, core), depth: 8 (over y_hi, z).
Axes of the slice: x: 4, y: 4 (y_hi: 2, y_lo: 2; y = y_hi * 2 + y_lo), z: 4, core: 2. Of those that a mesh axis runs over, the one named last changes fastest.
Arguments:
- positions: float32 [3, 16384, 128], P(None, ('box', 'depth')), may hold values from -0.5 to 0.5
- charges: float32 [2, 16384, 128], P(None, ('box', 'depth')), may hold values from -0.8 to 0.8
- counts: int32 [16384], P(('box', 'depth')), may hold values from 1 to 128
- owners: int32 [16384, 1], P(('box', 'depth')), may hold values from 0 to 127; in each aligned block of 128 rows (0 to 127, 128 to 255, ...) at most 2 rows name the same one
- leaves: int32 [16384], P(('box', 'depth')), may hold values from 0 to 255
- near_lists: int32 [64, 8, 4096], P(None, 'depth', 'box'), may hold values from 0 to 767
- image_lists: int32 [64, 8, 4096], P(None, 'depth', 'box'), may hold values from 0 to 767
- upward: float32 [304, 304], replicated, may hold values from -0.3125 to 0.3125
- child_ops: bfloat16 [304, 2432], replicated, may hold values from -0.125 to 0.125
- direct_ops: bfloat16 [19456, 304], replicated, may hold values from -0.0390625 to 0.0390625
- image_ops: bfloat16 [19456, 304], replicated, may hold values from -0.0390625 to 0.0390625
Outputs:
- potentials: float32 [304, 8, 4096], P(None, 'depth', 'box')
- parents: float32 [304, 8, 512], P(None, 'depth', 'box')
Inputs may be any that keep to these rules, and one draw needn't show every extreme that they name: `owners`: no device's 128 blocks name one owner more than 2 times, and some device's blocks name some owner exactly 2 times.
All inputs are finite; a program needn't handle non-finite values.
Results may differ from a plain program's by a relative error of at most 0.0029.
Values may be sent and summed in bfloat16 or wider, within the bound.
A program may use at most 128 MiB of HBM per device.

v0:
```python
import math
import jax
import jax.numpy as jnp
import numpy as np
from jax import lax
from jax.sharding import PartitionSpec as P

GRID = 6
wavenumber = 2.0


def extended(cells, sides, width):
    for axis, dim in sides:
        count = lax.axis_size(axis)
        ends = count - 1
        head = lax.slice_in_dim(cells, 0, width, axis=dim)
        tail = lax.slice_in_dim(cells, cells.shape[dim] - width, cells.shape[dim], axis=dim)
        cells = jnp.concatenate(
            [
                lax.ppermute(tail, axis, [(i, (i + 1) % count) for i in range(ends)]),
                cells,
                lax.ppermute(head, axis, [((i + 1) % count, i) for i in range(ends)]),
            ],
            axis=dim,
        )
    return cells


def swapped(block, axis, stride):
    count = lax.axis_size(axis)
    route = []
    for low in range(count):
        high = low | 1 << stride
        if high != low and high < count:
            route += [(low, high), (high, low)]
    return lax.ppermute(block, axis, route)


def surface_points(grid_size):
    indices = np.arange(grid_size)
    lattice = np.stack(np.meshgrid(indices, indices, indices, indexing="ij"), -1).reshape(-1, 3)
    outside = np.any((lattice == 0) | (lattice == grid_size - 1), axis=1)
    middle = (grid_size - 1) / 2.0
    return ((lattice[outside] - middle) * (1.5 / middle)).astype(np.float32)


def block_check(positions, charges):
    points = jnp.asarray(surface_points(GRID))
    delta_x = points[:, 0][:, None, None] - positions[0][None]
    delta_y = points[:, 1][:, None, None] - positions[1][None]
    delta_z = points[:, 2][:, None, None] - positions[2][None]
    radius = jnp.sqrt(delta_x * delta_x + delta_y * delta_y + delta_z * delta_z)
    cosine = jnp.cos(wavenumber * radius) / radius
    sine_part = jnp.sin(wavenumber * radius) / radius
    real_part = jnp.sum(cosine * charges[0][None] - sine_part * charges[1][None], axis=2)
    imaginary = jnp.sum(sine_part * charges[0][None] + cosine * charges[1][None], axis=2)
    return jnp.concatenate([real_part, imaginary], axis=0)


def checks_by_group(positions, charges):
    blocks = positions.shape[1]
    group_size = math.gcd(blocks, 32)
    group_count = blocks // group_size
    place_groups = positions.reshape(3, group_count, group_size, positions.shape[2]).transpose(
        1, 0, 2, 3
    )
    charge_groups = charges.reshape(2, group_count, group_size, charges.shape[2]).transpose(
        1, 0, 2, 3
    )

    def one_group(grouped):
        return block_check(grouped[0], grouped[1])

    values = lax.map(one_group, (place_groups, charge_groups))
    return values.transpose(1, 0, 2).reshape(values.shape[1], blocks)


def deliver(payload, leaf_row):
    return (
        lax.all_to_all(payload, ("box", "depth"), split_axis=1, concat_axis=1, tiled=True),
        lax.all_to_all(leaf_row, ("box", "depth"), split_axis=1, concat_axis=1, tiled=True),
    )


def translate(operators, window, lists):
    window_rows = window.T
    picked = lists[:, 0, :].T
    gathered = jnp.take(window_rows, picked, axis=0)
    flat = gathered.reshape(gathered.shape[0], -1)
    return jnp.dot(flat, operators, preferred_element_type=jnp.float32)


def local(
    positions,
    charges,
    counts,
    owners,
    leaves,
    near_lists,
    image_lists,
    upward,
    child_ops,
    direct_ops,
    image_ops,
):
    box_count = lax.axis_size("box")
    depth_count = lax.axis_size("depth")
    devices = box_count * depth_count
    blocks = positions.shape[1]
    row_count = positions.shape[2]
    capacity = 2 * blocks // devices
    slots = devices * capacity
    leaf_count = near_lists.shape[2]
    live = (jnp.arange(row_count, dtype=jnp.int32)[None, :] < counts[:, None]).astype(jnp.float32)
    masked = charges * live[None]
    target = owners[:, 0]
    order = jnp.arange(blocks, dtype=jnp.int32)
    earlier = (target[:, None] == target[None, :]) & (order[None, :] < order[:, None])
    slot_index = target * capacity + jnp.sum(earlier.astype(jnp.int32), axis=1)
    leaf_row = (
        jnp.full((1, slots), -1.0, jnp.float32).at[0, slot_index].set(leaves.astype(jnp.float32))
    )
    stacked = jnp.concatenate([positions, masked], axis=0)
    payload = jnp.zeros((5, slots, row_count), jnp.float32).at[:, slot_index, :].set(stacked)
    arrived, arrived_leaf = deliver(payload, leaf_row)
    block_values = checks_by_group(arrived[:3], arrived[3:])
    members = (
        arrived_leaf[0][:, None] == jnp.arange(leaf_count, dtype=jnp.float32)[None, :]
    ).astype(jnp.float32)
    check = jnp.dot(block_values, members, precision=lax.Precision.HIGHEST)
    multipole = jnp.dot(upward, check, precision=lax.Precision.HIGHEST).astype(jnp.bfloat16)
    channels = multipole.shape[0]
    children = (
        multipole.reshape(channels, leaf_count // 8, 8)
        .transpose(0, 2, 1)
        .reshape(channels * 8, leaf_count // 8)
    )
    parents = jnp.dot(child_ops, children, preferred_element_type=jnp.float32)
    window = extended(multipole, (("box", 1),), leaf_count)
    direct = translate(direct_ops, window, near_lists)
    bit_total = depth_count.bit_length() - 1
    mirrored = multipole
    for bit_number in range(bit_total):
        mirrored = swapped(mirrored, "depth", bit_number)
    image_window = extended(mirrored, (("box", 1),), leaf_count)
    reflected = translate(image_ops, image_window, image_lists)
    return ((direct + reflected).T[:, None, :], parents[:, None, :])


def solution(mesh):
    return jax.shard_map(
        local,
        mesh=mesh,
        in_specs=(
            P(None, ("box", "depth"), None),
            P(None, ("box", "depth"), None),
            P(("box", "depth")),
            P(("box", "depth"), None),
            P(("box", "depth")),
            P(None, "depth", "box"),
            P(None, "depth", "box"),
            P(),
            P(),
            P(),
            P(),
        ),
        out_specs=(P(None, "depth", "box"), P(None, "depth", "box")),
        check_vma=False,
    )
```

profile of v0, /device:TPU:9, one launch (start us, length us, event | category | flops | bytes accessed | tf_op | source)
XLA Modules:
  0.0 391.5 jit_solution(15532718104468842067)
XLA Ops:
  0.7 1.0 convert_reduce_fusion
  1.6 0.7 fusion.8
  2.3 0.7 convert_element_type.22
  3.0 1.0 scatter_custom_fusion.1
  3.9 0.8 all_to_all.10
  4.7 10.8 %all-to-all-start.1 = ((f32[1,128,2]{2,0,1:T(1,128)}), f32[1,128,2]{2,0,1:T(1,128)S(1)}, u32[]{:S(2)}, u32[]{:S(2)}) async-start(f32[1,128,2]{2,0,1:T(1,128)} %bitcast.11), calls=%async_computation.1 | async-start | bytes 131072 | tf_op jit(solution)/shard_map/all_to_all | solution.py:81
  15.5 0.7 fusion.7
  16.2 0.9 compare_select_fusion.1
  17.1 0.1 copy.54
  17.2 0.1 reshape.114
  17.3 0.9 compare_select_fusion
  18.2 0.9 broadcast_multiply_fusion
  19.1 1.0 maximum_bitcast_fusion.3
  20.1 0.2 copy.50
  20.3 0.1 copy.57
  20.5 1.0 broadcast_in_dim.38
  21.5 12.4 %scatter_fusion = f32[5,256,128]{2,0,1:T(8,128)} fusion(f32[5,256,128]{2,0,1:T(8,128)} %broadcast_in_dim.38, s32[128]{0:T(128)S(1)} %fusion.8, f32[128,5,128]{2,1,0:T(8,128)S(1)} %copy.50), kind=kCustom, calls=%fused_computation.2 | custom fusion | bytes 983552 | tf_op jit(solution)/shard_map/scatter | solution.py:124
  33.9 9.8 %all-to-all-start = ((f32[5,256,128]{2,0,1:T(8,128)}), f32[5,256,128]{2,0,1:T(8,128)S(1)}, u32[]{:S(2)}, u32[]{:S(2)}) async-start(f32[5,256,128]{2,0,1:T(8,128)} %scatter_fusion), calls=%async_computation | async-start | bytes 2097152 | tf_op jit(solution)/shard_map/all_to_all | solution.py:80
  43.8 0.5 broadcast.64
  44.3 0.8 reduce.3
  45.1 0.1 eq.34
  45.2 16.5 %all-to-all-done = f32[5,256,128]{2,0,1:T(8,128)S(1)} async-done(((f32[5,256,128]{2,0,1:T(8,128)}), f32[5,256,128]{2,0,1:T(8,128)S(1)}, u32[]{:S(2)}, u32[]{:S(2)}) %all-to-all-start) | async-done | bytes 655392 | tf_op jit(solution)/shard_map/all_to_all | solution.py:80
  61.7 0.1 slice.61
  61.8 0.1 slice.62
  62.0 108.3 %while.11 = (s32[]{:T(128)}, f32[8,304,32]{1,2,0:T(8,128)}, f32[8,3,32,128]{3,2,1,0:T(8,128)S(1)}, f32[8,2,32,128]{3,2,1,0:T(8,128)S(1)}, s32[]{:T(128)}, /*inde...) while((s32[]{:T(128)}, f32[8,304,32]{1,2,0:T(8,128)}, ...), condition=%wide.region_5.6_spmd.clone, body=%wide.region_2.5_spmd.sunk.clone.sunk | while | flops 11829252 | bytes 452541 | solution.py:74
  62.1 12.7 %subtract_reduce_fusion.2 = (f32[152,32]{1,0:T(8,128)S(1)}, f32[152,32]{1,0:T(8,128)S(1)}) fusion(f32[32,128]{1,0:T(8,128)S(1)} %get-tuple-element.104, f32[32,128]{1,0:T(8,128)S(1)} %get-tuple-element.105, f32[32,128]{1,0:T(8,128)S(1)} %get-tuple-element.106, f32[152]{0:T(256)S(1)} %get-tuple-element.141, f32[32,128]{1,0:T(8,128)S(1)} %get-tuple-element.107, ...), kind=kLoop, calls=%fused_computation.5.clone.1 | loop fusion | flops 11819520 | bytes 122656 | tf_op jit(solution)/shard_map/while/body/eval_jaxpr/reduce_sum | solution.py:55
  74.9 0.7 fusion.21
  75.6 12.7 %subtract_reduce_fusion.2 = (f32[152,32]{1,0:T(8,128)S(1)}, f32[152,32]{1,0:T(8,128)S(1)}) fusion(f32[32,128]{1,0:T(8,128)S(1)} %get-tuple-element.104, f32[32,128]{1,0:T(8,128)S(1)} %get-tuple-element.105, f32[32,128]{1,0:T(8,128)S(1)} %get-tuple-element.106, f32[152]{0:T(256)S(1)} %get-tuple-element.141, f32[32,128]{1,0:T(8,128)S(1)} %get-tuple-element.107, ...), kind=kLoop, calls=%fused_computation.5.clone.1 | loop fusion | flops 11819520 | bytes 122656 | tf_op jit(solution)/shard_map/while/body/eval_jaxpr/reduce_sum | solution.py:55
  88.4 0.7 fusion.21
  89.2 12.7 %subtract_reduce_fusion.2 = (f32[152,32]{1,0:T(8,128)S(1)}, f32[152,32]{1,0:T(8,128)S(1)}) fusion(f32[32,128]{1,0:T(8,128)S(1)} %get-tuple-element.104, f32[32,128]{1,0:T(8,128)S(1)} %get-tuple-element.105, f32[32,128]{1,0:T(8,128)S(1)} %get-tuple-element.106, f32[152]{0:T(256)S(1)} %get-tuple-element.141, f32[32,128]{1,0:T(8,128)S(1)} %get-tuple-element.107, ...), kind=kLoop, calls=%fused_computation.5.clone.1 | loop fusion | flops 11819520 | bytes 122656 | tf_op jit(solution)/shard_map/while/body/eval_jaxpr/reduce_sum | solution.py:55
  102.0 0.7 fusion.21
  102.7 12.7 %subtract_reduce_fusion.2 = (f32[152,32]{1,0:T(8,128)S(1)}, f32[152,32]{1,0:T(8,128)S(1)}) fusion(f32[32,128]{1,0:T(8,128)S(1)} %get-tuple-element.104, f32[32,128]{1,0:T(8,128)S(1)} %get-tuple-element.105, f32[32,128]{1,0:T(8,128)S(1)} %get-tuple-element.106, f32[152]{0:T(256)S(1)} %get-tuple-element.141, f32[32,128]{1,0:T(8,128)S(1)} %get-tuple-element.107, ...), kind=kLoop, calls=%fused_computation.5.clone.1 | loop fusion | flops 11819520 | bytes 122656 | tf_op jit(solution)/shard_map/while/body/eval_jaxpr/reduce_sum | solution.py:55
  115.5 0.7 fusion.21
  116.2 12.7 %subtract_reduce_fusion.2 = (f32[152,32]{1,0:T(8,128)S(1)}, f32[152,32]{1,0:T(8,128)S(1)}) fusion(f32[32,128]{1,0:T(8,128)S(1)} %get-tuple-element.104, f32[32,128]{1,0:T(8,128)S(1)} %get-tuple-element.105, f32[32,128]{1,0:T(8,128)S(1)} %get-tuple-element.106, f32[152]{0:T(256)S(1)} %get-tuple-element.141, f32[32,128]{1,0:T(8,128)S(1)} %get-tuple-element.107, ...), kind=kLoop, calls=%fused_computation.5.clone.1 | loop fusion | flops 11819520 | bytes 122656 | tf_op jit(solution)/shard_map/while/body/eval_jaxpr/reduce_sum | solution.py:55
  129.0 0.7 fusion.21
  129.8 12.7 %subtract_reduce_fusion.2 = (f32[152,32]{1,0:T(8,128)S(1)}, f32[152,32]{1,0:T(8,128)S(1)}) fusion(f32[32,128]{1,0:T(8,128)S(1)} %get-tuple-element.104, f32[32,128]{1,0:T(8,128)S(1)} %get-tuple-element.105, f32[32,128]{1,0:T(8,128)S(1)} %get-tuple-element.106, f32[152]{0:T(256)S(1)} %get-tuple-element.141, f32[32,128]{1,0:T(8,128)S(1)} %get-tuple-element.107, ...), kind=kLoop, calls=%fused_computation.5.clone.1 | loop fusion | flops 11819520 | bytes 122656 | tf_op jit(solution)/shard_map/while/body/eval_jaxpr/reduce_sum | solution.py:55
  142.6 0.7 fusion.21
  143.3 12.7 %subtract_reduce_fusion.2 = (f32[152,32]{1,0:T(8,128)S(1)}, f32[152,32]{1,0:T(8,128)S(1)}) fusion(f32[32,128]{1,0:T(8,128)S(1)} %get-tuple-element.104, f32[32,128]{1,0:T(8,128)S(1)} %get-tuple-element.105, f32[32,128]{1,0:T(8,128)S(1)} %get-tuple-element.106, f32[152]{0:T(256)S(1)} %get-tuple-element.141, f32[32,128]{1,0:T(8,128)S(1)} %get-tuple-element.107, ...), kind=kLoop, calls=%fused_computation.5.clone.1 | loop fusion | flops 11819520 | bytes 122656 | tf_op jit(solution)/shard_map/while/body/eval_jaxpr/reduce_sum | solution.py:55
  156.1 0.7 fusion.21
  156.8 12.7 %subtract_reduce_fusion.2 = (f32[152,32]{1,0:T(8,128)S(1)}, f32[152,32]{1,0:T(8,128)S(1)}) fusion(f32[32,128]{1,0:T(8,128)S(1)} %get-tuple-element.104, f32[32,128]{1,0:T(8,128)S(1)} %get-tuple-element.105, f32[32,128]{1,0:T(8,128)S(1)} %get-tuple-element.106, f32[152]{0:T(256)S(1)} %get-tuple-element.141, f32[32,128]{1,0:T(8,128)S(1)} %get-tuple-element.107, ...), kind=kLoop, calls=%fused_computation.5.clone.1 | loop fusion | flops 11819520 | bytes 122656 | tf_op jit(solution)/shard_map/while/body/eval_jaxpr/reduce_sum | solution.py:55
  169.6 0.7 fusion.21
  170.4 1.5 fusion.4
  171.9 0.7 fusion.2
  172.6 0.6 collective-permute-start.2
  173.2 2.5 collective-permute-start.1
  175.8 3.9 %collective-permute-start = (bf16[304,256]{1,0:T(8,128)(2,1)S(1)}, bf16[304,256]{1,0:T(8,128)(2,1)S(1)}, u32[]{:S(2)}, u32[]{:S(2)}) collective-permute-start(bf16[304,256]{1,0:T(8,128)(2,1)S(1)} %fusion.2), channel_id=1, source_target_pairs={{0,8},{8,16},{16,24},{24,32},{32,40},{40,48},{48,56},{56,64},{64,7... | collective-permute-start | bytes 466952 | tf_op jit(solution)/shard_map/ppermute | solution.py:20
  179.7 0.2 copy.60
  179.9 0.5 copy.61
  180.4 1.3 collective-permute-start.3
  181.6 1.2 convolution_bitcast_fusion
  182.9 0.3 copy.55
  183.2 65.6 %gather_fusion = bf16[16384,304]{1,0:T(8,128)(2,1)} fusion(bf16[768,304]{1,0:T(8,128)(2,1)S(1)} %copy.55, s32[16384]{0:T(1024)S(1)} %broadcast_clamp_fusion.1), kind=kCustom, calls=%fused_computation.clone | custom fusion | bytes 19988480 | tf_op jit(solution)/shard_map/jit(_take)/gather | solution.py:88
  248.7 15.8 %copy.56 = bf16[256,64,304]{0,2,1:T(8,128)(2,1)} copy(bf16[256,64,304]{2,1,0:T(8,128)(2,1)} %bitcast.84) | data formatting | bytes 19922944 | tf_op jit(solution)/shard_map/jit(_take)/gather | solution.py:88
  264.5 0.8 collective-permute-start.4
  265.3 8.5 %broadcast_select_fusion.1 = bf16[256,64,304]{0,2,1:T(8,128)(2,1)} fusion(bf16[256,64,304]{0,2,1:T(8,128)(2,1)} %copy.56, pred[256,64]{0,1:T(8,128)(4,1)S(1)} %compare_and_fusion.1), kind=kLoop, calls=%fused_computation.17 | loop fusion | flops 4980736 | bytes 19939328 | tf_op jit(solution)/shard_map/jit(_take)/select_n | solution.py:88
  273.8 3.0 collective-permute-start.6
  276.8 4.9 %collective-permute-start.5 = (bf16[304,256]{1,0:T(8,128)(2,1)S(1)}, bf16[304,256]{1,0:T(8,128)(2,1)S(1)}, u32[]{:S(2)}, u32[]{:S(2)}) collective-permute-start(bf16[304,256]{1,0:T(8,128)(2,1)S(1)} %collective-permute-done.4), channel_id=1, source_target_pairs={{0,8},{8,16},{16,24},{24,32},{32,40},{40,48},{48,56},{56,64},{64,7... | collective-permute-start | bytes 466952 | tf_op jit(solution)/shard_map/ppermute | solution.py:20
  281.7 9.2 %fusion.11 = f32[256,304]{0,1:T(8,128)S(1)} fusion(bf16[19456,304]{0,1:T(8,128)(2,1)} %param.25, bf16[256,19456]{0,1:T(8,128)(2,1)} %bitcast.86), kind=kOutput, calls=%fused_computation.49 | convolution fusion | flops 3028287488 | bytes 22102016 | tf_op jit(solution)/shard_map/dot_general | solution.py:90
  291.0 0.3 copy.58
  291.3 65.6 %gather_fusion.1 = bf16[16384,304]{1,0:T(8,128)(2,1)} fusion(bf16[768,304]{1,0:T(8,128)(2,1)S(1)} %copy.58, s32[16384]{0:T(1024)S(1)} %broadcast_clamp_fusion), kind=kCustom, calls=%fused_computation.1.clone | custom fusion | bytes 19988480 | tf_op jit(solution)/shard_map/jit(_take)/gather | solution.py:88
  356.9 15.8 %copy.59 = bf16[256,64,304]{0,2,1:T(8,128)(2,1)} copy(bf16[256,64,304]{2,1,0:T(8,128)(2,1)} %bitcast.85) | data formatting | bytes 19922944 | tf_op jit(solution)/shard_map/jit(_take)/gather | solution.py:88
  372.6 8.5 %broadcast_select_fusion = bf16[256,64,304]{0,2,1:T(8,128)(2,1)} fusion(bf16[256,64,304]{0,2,1:T(8,128)(2,1)} %copy.59, pred[256,64]{0,1:T(8,128)(4,1)S(1)} %compare_and_fusion), kind=kLoop, calls=%fused_computation.16 | loop fusion | flops 4980736 | bytes 19939328 | tf_op jit(solution)/shard_map/jit(_take)/select_n | solution.py:88
  381.2 9.3 %fusion.1 = f32[304,1,256]{2,0,1:T(8,128)S(1)} fusion(f32[256,304]{0,1:T(8,128)S(1)} %fusion.11, bf16[19456,304]{0,1:T(8,128)(2,1)} %param.26, bf16[256,19456]{0,1:T(8,128)(2,1)} %bitcast.87), kind=kOutput, calls=%fused_computation.19 | convolution fusion | flops 3028365312 | bytes 22413312 | tf_op jit(solution)/shard_map/dot_general | solution.py:90
  390.4 1.0 copy.62
  (58 shorter events, 1.5 us)
Async XLA Ops:
  0.6 181.0 %copy-start = (bf16[304,2432]{1,0:T(8,128)(2,1)S(1)}, bf16[304,2432]{1,0:T(8,128)(2,1)}, u32[]{:S(2)}) copy-start(bf16[304,2432]{1,0:T(8,128)(2,1)} %param.24) | copy-start | bytes 4435972
  0.6 43.1 %copy-start.3 = (s32[64,1,256]{2,1,0:T(1,128)S(1)}, s32[64,1,256]{2,1,0:T(1,128)}, u32[]{:S(2)}) copy-start(s32[64,1,256]{2,1,0:T(1,128)} %param.21) | copy-start | bytes 196612
  4.7 29.2 %all-to-all-start.1 = ((f32[1,128,2]{2,0,1:T(1,128)}), f32[1,128,2]{2,0,1:T(1,128)S(1)}, u32[]{:S(2)}, u32[]{:S(2)}) async-start(f32[1,128,2]{2,0,1:T(1,128)} %bitcast.11), calls=%async_computation.1 | async-start | bytes 131072 | tf_op jit(solution)/shard_map/all_to_all | solution.py:81
  17.3 44.7 %copy-start.5 = (f32[152]{0:T(256)S(1)}, f32[152]{0:T(256)}, u32[]{:S(2)}) copy-start(f32[152]{0:T(256)} %constant.98) | copy-start | bytes 1828
  17.3 44.7 %copy-start.6 = (f32[152]{0:T(256)S(1)}, f32[152]{0:T(256)}, u32[]{:S(2)}) copy-start(f32[152]{0:T(256)} %constant.99) | copy-start | bytes 1828
  17.3 44.7 %copy-start.7 = (f32[152]{0:T(256)S(1)}, f32[152]{0:T(256)}, u32[]{:S(2)}) copy-start(f32[152]{0:T(256)} %constant.100) | copy-start | bytes 1828
  33.9 27.7 %all-to-all-start = ((f32[5,256,128]{2,0,1:T(8,128)}), f32[5,256,128]{2,0,1:T(8,128)S(1)}, u32[]{:S(2)}, u32[]{:S(2)}) async-start(f32[5,256,128]{2,0,1:T(8,128)} %scatter_fusion), calls=%async_computation | async-start | bytes 2097152 | tf_op jit(solution)/shard_map/all_to_all | solution.py:80
  62.0 109.9 %copy-start.2 = (f32[304,304]{1,0:T(8,128)S(1)}, f32[304,304]{1,0:T(8,128)}, u32[]{:S(2)}) copy-start(f32[304,304]{1,0:T(8,128)} %param.23) | copy-start | bytes 1108996
  62.0 111.2 %copy-start.4 = (s32[64,1,256]{2,1,0:T(1,128)S(1)}, s32[64,1,256]{2,1,0:T(1,128)}, u32[]{:S(2)}) copy-start(s32[64,1,256]{2,1,0:T(1,128)} %param.22) | copy-start | bytes 196612
  172.6 7.8 %collective-permute-start.2 = (bf16[304,256]{1,0:T(8,128)(2,1)S(1)}, bf16[304,256]{1,0:T(8,128)(2,1)S(1)}, u32[]{:S(2)}, u32[]{:S(2)}) collective-permute-start(bf16[304,256]{1,0:T(8,128)(2,1)S(1)} %fusion.2), channel_id=1, source_target_pairs={{0,1},{1,0},{2,3},{3,2},{4,5},{5,4},{6,7},{7,6},{8,9},{9,8},{10,11... | collective-permute-start | bytes 466952 | tf_op jit(solution)/shard_map/ppermute | solution.py:36
  173.2 9.6 %collective-permute-start.1 = (bf16[304,256]{1,0:T(8,128)(2,1)S(1)}, bf16[304,256]{1,0:T(8,128)(2,1)S(1)}, u32[]{:S(2)}, u32[]{:S(2)}) collective-permute-start(bf16[304,256]{1,0:T(8,128)(2,1)S(1)} %fusion.2), channel_id=1, source_target_pairs={{8,0},{16,8},{24,16},{32,24},{40,32},{48,40},{56,48},{64,56},{72,6... | collective-permute-start | bytes 466952 | tf_op jit(solution)/shard_map/ppermute | solution.py:22
  175.8 7.1 %collective-permute-start = (bf16[304,256]{1,0:T(8,128)(2,1)S(1)}, bf16[304,256]{1,0:T(8,128)(2,1)S(1)}, u32[]{:S(2)}, u32[]{:S(2)}) collective-permute-start(bf16[304,256]{1,0:T(8,128)(2,1)S(1)} %fusion.2), channel_id=1, source_target_pairs={{0,8},{8,16},{16,24},{24,32},{32,40},{40,48},{48,56},{56,64},{64,7... | collective-permute-start | bytes 466952 | tf_op jit(solution)/shard_map/ppermute | solution.py:20
  180.4 84.2 %collective-permute-start.3 = (bf16[304,256]{1,0:T(8,128)(2,1)S(1)}, bf16[304,256]{1,0:T(8,128)(2,1)S(1)}, u32[]{:S(2)}, u32[]{:S(2)}) collective-permute-start(bf16[304,256]{1,0:T(8,128)(2,1)S(1)} %collective-permute-done.2), channel_id=1, source_target_pairs={{0,2},{2,0},{1,3},{3,1},{4,6},{6,4},{5,7},{7,5},{8,10},{10,8},{9,1... | collective-permute-start | bytes 466952 | tf_op jit(solution)/shard_map/ppermute | solution.py:36
  264.5 9.3 %collective-permute-start.4 = (bf16[304,256]{1,0:T(8,128)(2,1)S(1)}, bf16[304,256]{1,0:T(8,128)(2,1)S(1)}, u32[]{:S(2)}, u32[]{:S(2)}) collective-permute-start(bf16[304,256]{1,0:T(8,128)(2,1)S(1)} %collective-permute-done.3), channel_id=1, source_target_pairs={{0,4},{4,0},{1,5},{5,1},{2,6},{6,2},{3,7},{7,3},{8,12},{12,8},{9,1... | collective-permute-start | bytes 466952 | tf_op jit(solution)/shard_map/ppermute | solution.py:36
  273.8 17.1 %collective-permute-start.6 = (bf16[304,256]{1,0:T(8,128)(2,1)S(1)}, bf16[304,256]{1,0:T(8,128)(2,1)S(1)}, u32[]{:S(2)}, u32[]{:S(2)}) collective-permute-start(bf16[304,256]{1,0:T(8,128)(2,1)S(1)} %collective-permute-done.4), channel_id=1, source_target_pairs={{8,0},{16,8},{24,16},{32,24},{40,32},{48,40},{56,48},{64,56},{72,6... | collective-permute-start | bytes 466952 | tf_op jit(solution)/shard_map/ppermute | solution.py:22
  276.8 14.1 %collective-permute-start.5 = (bf16[304,256]{1,0:T(8,128)(2,1)S(1)}, bf16[304,256]{1,0:T(8,128)(2,1)S(1)}, u32[]{:S(2)}, u32[]{:S(2)}) collective-permute-start(bf16[304,256]{1,0:T(8,128)(2,1)S(1)} %collective-permute-done.4), channel_id=1, source_target_pairs={{0,8},{8,16},{16,24},{24,32},{32,40},{40,48},{48,56},{56,64},{64,7... | collective-permute-start | bytes 466952 | tf_op jit(solution)/shard_map/ppermute | solution.py:20
  381.2 10.3 %copy-start.1 = (bf16[304,2432]{1,0:T(8,128)(2,1)S(1)}, bf16[304,2432]{1,0:T(8,128)(2,1)}, u32[]{:S(2)}) copy-start(bf16[304,2432]{1,0:T(8,128)(2,1)} %param.24) | copy-start | bytes 4435972
where the time goes:
time: 393 us; the launch traced here: 391 us
  local copies, waits for them, and re-layouts  183 us (47%)
  other arithmetic  132 us (34%)
  starting transfers between devices  37.5 us (10%)
  matrix products  21.8 us (6%)
  waiting for transfers between devices  16.5 us (4%)
    gather x4, local copies, waits for them, and re-layouts, translate(): gathered = jnp.take(window_rows, picked, axis=0)  163 us
    reduce_sum x8, other arithmetic, block_check(): jnp.sum(cosine * charges[0][None] - sine_part * charges[1][None], axis=2)  101 us
    select_n x4, other arithmetic, translate(): gathered = jnp.take(window_rows, picked, axis=0)  18.8 us
    dot_general x2, matrix products, translate(): return jnp.dot(flat, operators, preferred_element_type=jnp.float32)  18.4 us
    all_to_all x1, waiting for transfers between devices, deliver(): lax.all_to_all(payload, ('box', 'depth'), split_axis=1, concat_axis=1, ti...  16.5 us
    scatter x1, local copies, waits for them, and re-layouts, local(): jnp.zeros((5, slots, row_count), jnp.float32).at[:, slot_index, :]  12.4 us
    all_to_all x1, starting transfers between devices, deliver(): lax.all_to_all(leaf_row, ('box', 'depth'), split_axis=1, concat_axis=1, t...  10.8 us
    all_to_all x1, starting transfers between devices, deliver(): lax.all_to_all(payload, ('box', 'depth'), split_axis=1, concat_axis=1, ti...  9.75 us
  transfers between devices with their start and end apart: 9, of which 1 were waited for; matrix products, arithmetic and copies ran while one was open for 31% of the time, Pallas kernels for 0%

commit v1 on v0

--- a/solution.py
+++ b/solution.py
@@ -77,7 +77,15 @@
 
 def deliver(payload, leaf_row):
     return (
-        lax.all_to_all(payload, ("box", "depth"), split_axis=1, concat_axis=1, tiled=True),
+        jnp.concatenate(
+            lax.all_to_all(
+                jnp.stack(jnp.split(payload, lax.axis_size(("box", "depth")), axis=1)),
+                ("box", "depth"),
+                0,
+                0,
+            ),
+            axis=1,
+        ),
         lax.all_to_all(leaf_row, ("box", "depth"), split_axis=1, concat_axis=1, tiled=True),
     )
 

time: 393 us -> 451 us (1.15)
  local copies, waits for them, and re-layouts: 183 us -> 252 us
  other arithmetic: 132 us -> 126 us
  waiting for transfers between devices: 16.5 us -> 11.8 us
    unnamed x17 -> x146, local copies, waits for them, and re-layouts: 1.09 us -> 76.6 us
    scatter x1, local copies, waits for them, and re-layouts: 12.4 us -> 4.3 us  [local(): jnp.zeros((5, slots, row_count), jnp.float32).at[:, slot_index, :]]
    dynamic_update_slice x8, other arithmetic: 5.63 us -> 0.67 us  [checks_by_group(): values = lax.map(one_group, (place_groups, charge_groups))]
    all_to_all x1, waiting for transfers between devices: 16.5 us -> 11.8 us  [deliver(): lax.all_to_all(jnp.stack(jnp.split(payload, lax.axis_size(('box', 'depth'...]
  transfers between devices with their start and end apart: 9 -> 9, of which waited for: 1 -> 1; matrix products, arithmetic and copies ran while one was open for 31% -> 42% of each run, Pallas kernels for 0% -> 0%
where the time goes in v1:
time: 451 us; the launch traced here: 450 us
  local copies, waits for them, and re-layouts  252 us (56%)
  other arithmetic  126 us (28%)
  starting transfers between devices  37.8 us (8%)
  matrix products  20.8 us (5%)
  waiting for transfers between devices  11.8 us (3%)
    gather x4, local copies, waits for them, and re-layouts, translate(): gathered = jnp.take(window_rows, picked, axis=0)  162 us
    reduce_sum x8, other arithmetic, block_check(): jnp.sum(cosine * charges[0][None] - sine_part * charges[1][None], axis=2)  101 us
    unnamed x146, local copies, waits for them, and re-layouts  76.6 us
    dot_general x2, matrix products, translate(): return jnp.dot(flat, operators, preferred_element_type=jnp.float32)  18.4 us
    select_n x4, other arithmetic, translate(): gathered = jnp.take(window_rows, picked, axis=0)  17.1 us
    all_to_all x1, waiting for transfers between devices, deliver(): lax.all_to_all(jnp.stack(jnp.split(payload, lax.axis_size(('box', 'depth'...  11.8 us
    all_to_all x1, starting transfers between devices, deliver(): lax.all_to_all(leaf_row, ('box', 'depth'), split_axis=1, concat_axis=1, t...  11.2 us
    all_to_all x1, starting transfers between devices, deliver(): lax.all_to_all(jnp.stack(jnp.split(payload, lax.axis_size(('box', 'depth'...  9.77 us
  transfers between devices with their start and end apart: 9, of which 1 were waited for; matrix products, arithmetic and copies ran while one was open for 42% of the time, Pallas kernels for 0%

profile of v1, /device:TPU:9, one launch (start us, length us, event | category | flops | bytes accessed | tf_op | source)
XLA Modules:
  0.0 449.5 jit_solution(2855506395393984190)
XLA Ops:
  0.7 1.0 convert_reduce_fusion
  1.6 0.7 fusion.8
  2.3 0.7 convert_element_type.22
  3.0 1.0 scatter_custom_fusion.1
  3.9 0.8 all_to_all.10
  4.7 11.2 %all-to-all-start.1 = ((f32[1,128,2]{2,0,1:T(1,128)}), f32[1,128,2]{2,0,1:T(1,128)}, u32[]{:S(2)}, u32[]{:S(2)}) async-start(f32[1,128,2]{2,0,1:T(1,128)} %bitcast.140), calls=%async_computation.1 | async-start | bytes 131072 | tf_op jit(solution)/shard_map/all_to_all | solution.py:89
  15.9 0.7 fusion.7
  16.7 0.9 broadcast_multiply_fusion
  17.6 1.0 maximum_bitcast_fusion.3
  18.9 4.3 scatter_fusion
  27.4 0.6 constant_dynamic-update-slice_fusion.120
  30.9 0.6 constant_dynamic-update-slice_fusion.114
  35.1 0.6 constant_dynamic-update-slice_fusion.107
  36.9 0.6 constant_dynamic-update-slice_fusion.104
  38.7 0.6 constant_dynamic-update-slice_fusion.101
  40.5 0.6 constant_dynamic-update-slice_fusion.98
  44.6 0.6 constant_dynamic-update-slice_fusion.91
  47.6 0.6 constant_dynamic-update-slice_fusion.86
  53.6 0.6 constant_dynamic-update-slice_fusion.76
  54.7 0.6 constant_dynamic-update-slice_fusion.74
  55.9 0.6 constant_dynamic-update-slice_fusion.72
  64.8 0.6 constant_dynamic-update-slice_fusion.57
  76.1 0.6 constant_dynamic-update-slice_fusion.38
  79.7 0.6 constant_dynamic-update-slice_fusion.32
  82.1 0.6 constant_dynamic-update-slice_fusion.28
  86.8 0.6 constant_dynamic-update-slice_fusion.20
  87.4 0.6 constant_dynamic-update-slice_fusion.19
  91.0 0.6 constant_dynamic-update-slice_fusion.13
  93.4 0.6 constant_dynamic-update-slice_fusion.9
  94.0 0.6 constant_dynamic-update-slice_fusion.8
  94.6 0.6 constant_dynamic-update-slice_fusion.7
  97.6 0.6 constant_dynamic-update-slice_fusion.2
  99.0 0.6 constant_dynamic-update-slice_fusion
  99.6 2.4 copy.66
  102.3 9.8 %all-to-all-start = ((f32[128,5,2,128]{3,2,1,0:T(2,128)}), f32[128,5,2,128]{3,2,1,0:T(2,128)S(1)}, u32[]{:S(2)}, u32[]{:S(2)}) async-start(f32[128,5,2,128]{3,2,1,0:T(2,128)} %copy.66), calls=%async_computation | async-start | bytes 1310720 | tf_op jit(solution)/shard_map/all_to_all | solution.py:81
  112.6 1.7 reduce.3
  114.4 11.8 %all-to-all-done = f32[128,5,2,128]{3,2,1,0:T(2,128)S(1)} async-done(((f32[128,5,2,128]{3,2,1,0:T(2,128)}), f32[128,5,2,128]{3,2,1,0:T(2,128)S(1)}, u32[]{:S(2)}, u32[]{:S(2)}) %all-to-all-start) | async-done | bytes 655392 | tf_op jit(solution)/shard_map/all_to_all | solution.py:81
  126.6 103.6 %while.11 = (s32[]{:T(128)}, f32[8,304,32]{1,2,0:T(8,128)S(1)}, f32[8,3,32,128]{3,2,0,1:T(8,128)S(1)}, f32[8,2,32,128]{3,2,0,1:T(8,128)S(1)}, s32[]{:T(128)}, /*...) while((s32[]{:T(128)}, f32[8,304,32]{1,2,0:T(8,128)S(1)}, ...), condition=%wide.region_5.6_spmd.clone, body=%wide.region_2.5_spmd.sunk.clone.sunk | while | flops 11829250 | bytes 642953 | solution.py:74
  126.7 12.7 %subtract_reduce_fusion.2 = (f32[152,32]{1,0:T(8,128)S(1)}, f32[152,32]{1,0:T(8,128)S(1)}) fusion(f32[32,128]{1,0:T(8,128)S(1)} %get-tuple-element.114, f32[32,128]{1,0:T(8,128)S(1)} %get-tuple-element.115, f32[32,128]{1,0:T(8,128)S(1)} %get-tuple-element.116, f32[152]{0:T(256)S(1)} %get-tuple-element.142, f32[32,128]{1,0:T(8,128)S(1)} %get-tuple-element.117, ...), kind=kLoop, calls=%fused_computation.5.clone.1 | loop fusion | flops 11819520 | bytes 122656 | tf_op jit(solution)/shard_map/while/body/eval_jaxpr/reduce_sum | solution.py:55
  139.7 12.7 %subtract_reduce_fusion.2 = (f32[152,32]{1,0:T(8,128)S(1)}, f32[152,32]{1,0:T(8,128)S(1)}) fusion(f32[32,128]{1,0:T(8,128)S(1)} %get-tuple-element.114, f32[32,128]{1,0:T(8,128)S(1)} %get-tuple-element.115, f32[32,128]{1,0:T(8,128)S(1)} %get-tuple-element.116, f32[152]{0:T(256)S(1)} %get-tuple-element.142, f32[32,128]{1,0:T(8,128)S(1)} %get-tuple-element.117, ...), kind=kLoop, calls=%fused_computation.5.clone.1 | loop fusion | flops 11819520 | bytes 122656 | tf_op jit(solution)/shard_map/while/body/eval_jaxpr/reduce_sum | solution.py:55
  152.6 12.7 %subtract_reduce_fusion.2 = (f32[152,32]{1,0:T(8,128)S(1)}, f32[152,32]{1,0:T(8,128)S(1)}) fusion(f32[32,128]{1,0:T(8,128)S(1)} %get-tuple-element.114, f32[32,128]{1,0:T(8,128)S(1)} %get-tuple-element.115, f32[32,128]{1,0:T(8,128)S(1)} %get-tuple-element.116, f32[152]{0:T(256)S(1)} %get-tuple-element.142, f32[32,128]{1,0:T(8,128)S(1)} %get-tuple-element.117, ...), kind=kLoop, calls=%fused_computation.5.clone.1 | loop fusion | flops 11819520 | bytes 122656 | tf_op jit(solution)/shard_map/while/body/eval_jaxpr/reduce_sum | solution.py:55
  165.6 12.7 %subtract_reduce_fusion.2 = (f32[152,32]{1,0:T(8,128)S(1)}, f32[152,32]{1,0:T(8,128)S(1)}) fusion(f32[32,128]{1,0:T(8,128)S(1)} %get-tuple-element.114, f32[32,128]{1,0:T(8,128)S(1)} %get-tuple-element.115, f32[32,128]{1,0:T(8,128)S(1)} %get-tuple-element.116, f32[152]{0:T(256)S(1)} %get-tuple-element.142, f32[32,128]{1,0:T(8,128)S(1)} %get-tuple-element.117, ...), kind=kLoop, calls=%fused_computation.5.clone.1 | loop fusion | flops 11819520 | bytes 122656 | tf_op jit(solution)/shard_map/while/body/eval_jaxpr/reduce_sum | solution.py:55
  178.5 12.7 %subtract_reduce_fusion.2 = (f32[152,32]{1,0:T(8,128)S(1)}, f32[152,32]{1,0:T(8,128)S(1)}) fusion(f32[32,128]{1,0:T(8,128)S(1)} %get-tuple-element.114, f32[32,128]{1,0:T(8,128)S(1)} %get-tuple-element.115, f32[32,128]{1,0:T(8,128)S(1)} %get-tuple-element.116, f32[152]{0:T(256)S(1)} %get-tuple-element.142, f32[32,128]{1,0:T(8,128)S(1)} %get-tuple-element.117, ...), kind=kLoop, calls=%fused_computation.5.clone.1 | loop fusion | flops 11819520 | bytes 122656 | tf_op jit(solution)/shard_map/while/body/eval_jaxpr/reduce_sum | solution.py:55
  191.5 12.7 %subtract_reduce_fusion.2 = (f32[152,32]{1,0:T(8,128)S(1)}, f32[152,32]{1,0:T(8,128)S(1)}) fusion(f32[32,128]{1,0:T(8,128)S(1)} %get-tuple-element.114, f32[32,128]{1,0:T(8,128)S(1)} %get-tuple-element.115, f32[32,128]{1,0:T(8,128)S(1)} %get-tuple-element.116, f32[152]{0:T(256)S(1)} %get-tuple-element.142, f32[32,128]{1,0:T(8,128)S(1)} %get-tuple-element.117, ...), kind=kLoop, calls=%fused_computation.5.clone.1 | loop fusion | flops 11819520 | bytes 122656 | tf_op jit(solution)/shard_map/while/body/eval_jaxpr/reduce_sum | solution.py:55
  204.4 12.7 %subtract_reduce_fusion.2 = (f32[152,32]{1,0:T(8,128)S(1)}, f32[152,32]{1,0:T(8,128)S(1)}) fusion(f32[32,128]{1,0:T(8,128)S(1)} %get-tuple-element.114, f32[32,128]{1,0:T(8,128)S(1)} %get-tuple-element.115, f32[32,128]{1,0:T(8,128)S(1)} %get-tuple-element.116, f32[152]{0:T(256)S(1)} %get-tuple-element.142, f32[32,128]{1,0:T(8,128)S(1)} %get-tuple-element.117, ...), kind=kLoop, calls=%fused_computation.5.clone.1 | loop fusion | flops 11819520 | bytes 122656 | tf_op jit(solution)/shard_map/while/body/eval_jaxpr/reduce_sum | solution.py:55
  217.4 12.7 %subtract_reduce_fusion.2 = (f32[152,32]{1,0:T(8,128)S(1)}, f32[152,32]{1,0:T(8,128)S(1)}) fusion(f32[32,128]{1,0:T(8,128)S(1)} %get-tuple-element.114, f32[32,128]{1,0:T(8,128)S(1)} %get-tuple-element.115, f32[32,128]{1,0:T(8,128)S(1)} %get-tuple-element.116, f32[152]{0:T(256)S(1)} %get-tuple-element.142, f32[32,128]{1,0:T(8,128)S(1)} %get-tuple-element.117, ...), kind=kLoop, calls=%fused_computation.5.clone.1 | loop fusion | flops 11819520 | bytes 122656 | tf_op jit(solution)/shard_map/while/body/eval_jaxpr/reduce_sum | solution.py:55
  230.8 0.7 fusion.2
  231.5 0.6 collective-permute-start.2
  232.2 2.1 collective-permute-start.1
  234.3 4.4 collective-permute-start
  239.3 1.0 collective-permute-start.3
  240.3 1.2 convolution_bitcast_fusion
  241.8 65.3 %gather_fusion = bf16[16384,304]{1,0:T(8,128)(2,1)} fusion(bf16[768,304]{1,0:T(8,128)(2,1)S(1)} %copy.73, s32[16384]{0:T(1024)S(1)} %broadcast_clamp_fusion.1), kind=kCustom, calls=%fused_computation.clone | custom fusion | bytes 19988480 | tf_op jit(solution)/shard_map/jit(_take)/gather | solution.py:96
  307.1 15.8 %copy.74 = bf16[256,64,304]{0,2,1:T(8,128)(2,1)} copy(bf16[256,64,304]{2,1,0:T(8,128)(2,1)} %bitcast.603) | data formatting | bytes 19922944 | tf_op jit(solution)/shard_map/jit(_take)/gather | solution.py:96
  322.8 1.0 collective-permute-start.4
  323.9 8.5 %broadcast_select_fusion.1 = bf16[256,64,304]{0,2,1:T(8,128)(2,1)} fusion(bf16[256,64,304]{0,2,1:T(8,128)(2,1)} %copy.74, pred[256,64]{0,1:T(8,128)(4,1)S(1)} %compare_and_fusion.1), kind=kLoop, calls=%fused_computation.19 | loop fusion | flops 4980736 | bytes 19939328 | tf_op jit(solution)/shard_map/jit(_take)/select_n | solution.py:96
  332.4 2.9 collective-permute-start.6
  335.4 4.7 %collective-permute-start.5 = (bf16[304,256]{1,0:T(8,128)(2,1)S(1)}, bf16[304,256]{1,0:T(8,128)(2,1)S(1)}, u32[]{:S(2)}, u32[]{:S(2)}) collective-permute-start(bf16[304,256]{1,0:T(8,128)(2,1)S(1)} %collective-permute-done.4), channel_id=1, source_target_pairs={{0,8},{8,16},{16,24},{24,32},{32,40},{40,48},{48,56},{56,64},{64,7... | collective-permute-start | bytes 466952 | tf_op jit(solution)/shard_map/ppermute | solution.py:20
  340.1 9.2 %fusion.11 = f32[256,304]{0,1:T(8,128)S(1)} fusion(bf16[19456,304]{0,1:T(8,128)(2,1)} %param.25, bf16[256,19456]{0,1:T(8,128)(2,1)} %bitcast.605), kind=kOutput, calls=%fused_computation.305 | convolution fusion | flops 3028287488 | bytes 22102016 | tf_op jit(solution)/shard_map/dot_general | solution.py:98
  349.6 65.3 %gather_fusion.1 = bf16[16384,304]{1,0:T(8,128)(2,1)} fusion(bf16[768,304]{1,0:T(8,128)(2,1)S(1)} %copy.76, s32[16384]{0:T(1024)S(1)} %broadcast_clamp_fusion), kind=kCustom, calls=%fused_computation.1.clone | custom fusion | bytes 19988480 | tf_op jit(solution)/shard_map/jit(_take)/gather | solution.py:96
  414.9 15.8 %copy.77 = bf16[256,64,304]{0,2,1:T(8,128)(2,1)} copy(bf16[256,64,304]{2,1,0:T(8,128)(2,1)} %bitcast.604) | data formatting | bytes 19922944 | tf_op jit(solution)/shard_map/jit(_take)/gather | solution.py:96
  430.7 8.5 %broadcast_select_fusion = bf16[256,64,304]{0,2,1:T(8,128)(2,1)} fusion(bf16[256,64,304]{0,2,1:T(8,128)(2,1)} %copy.77, pred[256,64]{0,1:T(8,128)(4,1)S(1)} %compare_and_fusion), kind=kLoop, calls=%fused_computation.18 | loop fusion | flops 4980736 | bytes 19939328 | tf_op jit(solution)/shard_map/jit(_take)/select_n | solution.py:96
  439.2 9.3 %fusion.1 = f32[304,1,256]{2,0,1:T(8,128)S(1)} fusion(f32[256,304]{0,1:T(8,128)S(1)} %fusion.11, bf16[19456,304]{0,1:T(8,128)(2,1)} %param.26, bf16[256,19456]{0,1:T(8,128)(2,1)} %bitcast.606), kind=kOutput, calls=%fused_computation.21 | convolution fusion | flops 3028365312 | bytes 22413312 | tf_op jit(solution)/shard_map/dot_general | solution.py:98
  448.5 1.0 copy.80
  (205 shorter events, 67.9 us)
Async XLA Ops:
  0.6 239.6 %copy-start = (bf16[304,2432]{1,0:T(8,128)(2,1)S(1)}, bf16[304,2432]{1,0:T(8,128)(2,1)}, u32[]{:S(2)}) copy-start(bf16[304,2432]{1,0:T(8,128)(2,1)} %param.24) | copy-start | bytes 4435972
  0.6 98.1 %copy-start.3 = (s32[64,1,256]{2,1,0:T(1,128)S(1)}, s32[64,1,256]{2,1,0:T(1,128)}, u32[]{:S(2)}) copy-start(s32[64,1,256]{2,1,0:T(1,128)} %param.21) | copy-start | bytes 196612
  0.7 98.3 %copy-start.4 = (s32[64,1,256]{2,1,0:T(1,128)S(1)}, s32[64,1,256]{2,1,0:T(1,128)}, u32[]{:S(2)}) copy-start(s32[64,1,256]{2,1,0:T(1,128)} %param.22) | copy-start | bytes 196612
  4.7 97.6 %all-to-all-start.1 = ((f32[1,128,2]{2,0,1:T(1,128)}), f32[1,128,2]{2,0,1:T(1,128)}, u32[]{:S(2)}, u32[]{:S(2)}) async-start(f32[1,128,2]{2,0,1:T(1,128)} %bitcast.140), calls=%async_computation.1 | async-start | bytes 131072 | tf_op jit(solution)/shard_map/all_to_all | solution.py:89
  18.9 107.7 %copy-start.6 = (f32[152]{0:T(256)S(1)}, f32[152]{0:T(256)}, u32[]{:S(2)}) copy-start(f32[152]{0:T(256)} %constant.604) | copy-start | bytes 1828
  18.9 107.7 %copy-start.7 = (f32[152]{0:T(256)S(1)}, f32[152]{0:T(256)}, u32[]{:S(2)}) copy-start(f32[152]{0:T(256)} %constant.605) | copy-start | bytes 1828
  18.9 107.7 %copy-start.8 = (f32[152]{0:T(256)S(1)}, f32[152]{0:T(256)}, u32[]{:S(2)}) copy-start(f32[152]{0:T(256)} %constant.606) | copy-start | bytes 1828
  102.3 23.9 %all-to-all-start = ((f32[128,5,2,128]{3,2,1,0:T(2,128)}), f32[128,5,2,128]{3,2,1,0:T(2,128)S(1)}, u32[]{:S(2)}, u32[]{:S(2)}) async-start(f32[128,5,2,128]{3,2,1,0:T(2,128)} %copy.66), calls=%async_computation | async-start | bytes 1310720 | tf_op jit(solution)/shard_map/all_to_all | solution.py:81
  126.6 104.2 %copy-start.2 = (f32[304,304]{1,0:T(8,128)S(1)}, f32[304,304]{1,0:T(8,128)}, u32[]{:S(2)}) copy-start(f32[304,304]{1,0:T(8,128)} %param.23) | copy-start | bytes 1108996
  126.6 105.5 %copy-start.5 = (s32[64,1,256]{2,1,0:T(1,128)S(1)}, s32[64,1,256]{2,1,0:T(1,128)}, u32[]{:S(2)}) copy-start(s32[64,1,256]{2,1,0:T(1,128)} %param.22) | copy-start | bytes 196612
  231.5 7.8 %collective-permute-start.2 = (bf16[304,256]{1,0:T(8,128)(2,1)S(1)}, bf16[304,256]{1,0:T(8,128)(2,1)S(1)}, u32[]{:S(2)}, u32[]{:S(2)}) collective-permute-start(bf16[304,256]{1,0:T(8,128)(2,1)S(1)} %fusion.2), channel_id=1, source_target_pairs={{0,1},{1,0},{2,3},{3,2},{4,5},{5,4},{6,7},{7,6},{8,9},{9,8},{10,11... | collective-permute-start | bytes 466952 | tf_op jit(solution)/shard_map/ppermute | solution.py:36
  232.2 9.3 %collective-permute-start.1 = (bf16[304,256]{1,0:T(8,128)(2,1)S(1)}, bf16[304,256]{1,0:T(8,128)(2,1)S(1)}, u32[]{:S(2)}, u32[]{:S(2)}) collective-permute-start(bf16[304,256]{1,0:T(8,128)(2,1)S(1)} %fusion.2), channel_id=1, source_target_pairs={{8,0},{16,8},{24,16},{32,24},{40,32},{48,40},{56,48},{64,56},{72,6... | collective-permute-start | bytes 466952 | tf_op jit(solution)/shard_map/ppermute | solution.py:22
  234.3 7.2 %collective-permute-start = (bf16[304,256]{1,0:T(8,128)(2,1)S(1)}, bf16[304,256]{1,0:T(8,128)(2,1)S(1)}, u32[]{:S(2)}, u32[]{:S(2)}) collective-permute-start(bf16[304,256]{1,0:T(8,128)(2,1)S(1)} %fusion.2), channel_id=1, source_target_pairs={{0,8},{8,16},{16,24},{24,32},{32,40},{40,48},{48,56},{56,64},{64,7... | collective-permute-start | bytes 466952 | tf_op jit(solution)/shard_map/ppermute | solution.py:20
  239.3 83.5 %collective-permute-start.3 = (bf16[304,256]{1,0:T(8,128)(2,1)S(1)}, bf16[304,256]{1,0:T(8,128)(2,1)S(1)}, u32[]{:S(2)}, u32[]{:S(2)}) collective-permute-start(bf16[304,256]{1,0:T(8,128)(2,1)S(1)} %collective-permute-done.2), channel_id=1, source_target_pairs={{0,2},{2,0},{1,3},{3,1},{4,6},{6,4},{5,7},{7,5},{8,10},{10,8},{9,1... | collective-permute-start | bytes 466952 | tf_op jit(solution)/shard_map/ppermute | solution.py:36
  322.8 9.6 %collective-permute-start.4 = (bf16[304,256]{1,0:T(8,128)(2,1)S(1)}, bf16[304,256]{1,0:T(8,128)(2,1)S(1)}, u32[]{:S(2)}, u32[]{:S(2)}) collective-permute-start(bf16[304,256]{1,0:T(8,128)(2,1)S(1)} %collective-permute-done.3), channel_id=1, source_target_pairs={{0,4},{4,0},{1,5},{5,1},{2,6},{6,2},{3,7},{7,3},{8,12},{12,8},{9,1... | collective-permute-start | bytes 466952 | tf_op jit(solution)/shard_map/ppermute | solution.py:36
  332.4 16.9 %collective-permute-start.6 = (bf16[304,256]{1,0:T(8,128)(2,1)S(1)}, bf16[304,256]{1,0:T(8,128)(2,1)S(1)}, u32[]{:S(2)}, u32[]{:S(2)}) collective-permute-start(bf16[304,256]{1,0:T(8,128)(2,1)S(1)} %collective-permute-done.4), channel_id=1, source_target_pairs={{8,0},{16,8},{24,16},{32,24},{40,32},{48,40},{56,48},{64,56},{72,6... | collective-permute-start | bytes 466952 | tf_op jit(solution)/shard_map/ppermute | solution.py:22
  335.4 13.9 %collective-permute-start.5 = (bf16[304,256]{1,0:T(8,128)(2,1)S(1)}, bf16[304,256]{1,0:T(8,128)(2,1)S(1)}, u32[]{:S(2)}, u32[]{:S(2)}) collective-permute-start(bf16[304,256]{1,0:T(8,128)(2,1)S(1)} %collective-permute-done.4), channel_id=1, source_target_pairs={{0,8},{8,16},{16,24},{24,32},{32,40},{40,48},{48,56},{56,64},{64,7... | collective-permute-start | bytes 466952 | tf_op jit(solution)/shard_map/ppermute | solution.py:20
  439.2 10.3 %copy-start.1 = (bf16[304,2432]{1,0:T(8,128)(2,1)S(1)}, bf16[304,2432]{1,0:T(8,128)(2,1)}, u32[]{:S(2)}) copy-start(bf16[304,2432]{1,0:T(8,128)(2,1)} %param.24) | copy-start | bytes 4435972
